TPU v7x, 32 devices: a whole 2x2x4 slice. The times are simulated.
32 devices in a mesh: pb: 8 (over y, x, core), row: 4 (over z).
Axes of the slice: x: 2, y: 2, z: 4, core: 2. Of those that a mesh axis runs over, the one named last changes fastest.
Arguments:
- valence_bands: bfloat16 [8, 20, 4096], P('pb', None, 'row'), may hold values from -0.75 to 0.75
- conduction_bands: bfloat16 [8, 20, 4096], P('pb', None, 'row'), may hold values from -6 to 6
- screened: bfloat16 [8, 4096, 4096], P('pb', 'row'), may hold values from -0.09375 to 0.09375
- pair_list: int32 [16, 2], replicated, may hold values from 0 to 7, as said below
- transfer_index: int32 [16, 1], replicated, may hold values from 0 to 7; in each aligned block of 16 rows (0 to 15, 16 to 31, ...) at most 6 rows name the same one
- owner_map: int32 [8], replicated, may hold values from 0 to 7, as said below
Outputs:
- direct: bfloat16 [16, 400, 400], P('pb', 'row')
- mirror: bfloat16 [16, 400, 400], P('pb', 'row')
Inputs may be any that keep to these rules, and one draw needn't show every extreme that they name: owner_map is a permutation of 0 to 7. `pair_list`: the two k-points of a pair differ. The first k-point of pairs e * 2 to e * 2 + 1 is the one that owner_map sends to e. Over all pairs, the second k-points are sent by owner_map to every value 0 to 7 exactly 2 times. `transfer_index`: at most 6 pairs share one momentum transfer, and some transfer has exactly 6; every transfer has at least one pair.
All inputs are finite; a program needn't handle non-finite values.
Results may differ from a plain program's by a relative error of at most 0.0065.
Values may be sent and summed in bfloat16 or wider, within the bound.
No kernel may reach another device: no remote copies, remote signals or barrier semaphores. Data moves between devices by JAX's collectives and lax.ppermute only.
A program may use at most 64 MiB of HBM per device.

v0:
```python
import jax
import jax.numpy as jnp
from jax import lax
from jax.sharding import PartitionSpec as P

PAIR_DEV = 2
MOST = 6


def rank_table(labels, groups, slots_per):
    total_rows = labels.shape[0]
    member = (labels[None, :] == jnp.arange(groups, dtype=jnp.int32)[:, None]).astype(jnp.int32)
    before = jnp.cumsum(member, axis=1) - 1
    placed = member[:, None, :] * (
        before[:, None, :] == jnp.arange(slots_per, dtype=jnp.int32)[None, :, None]
    ).astype(jnp.int32)
    numbers = jnp.arange(total_rows, dtype=jnp.int32) + 1
    return jnp.sum(placed * numbers[None, None, :], axis=2) - 1


def pair_kernel(val_first, val_second, con_first, con_second, screen_rows):
    val_count = val_first.shape[0]
    con_count = con_first.shape[0]
    val_pairs = val_first[:, None, :].astype(jnp.float32) * val_second[None, :, :].astype(
        jnp.float32
    )
    val_pairs = val_pairs.reshape(val_count * val_count, val_first.shape[1]).astype(jnp.bfloat16)
    con_pairs = con_first[:, None, :].astype(jnp.float32) * con_second[None, :, :].astype(
        jnp.float32
    )
    con_pairs = con_pairs.reshape(con_count * con_count, con_first.shape[1]).astype(jnp.bfloat16)
    interim = lax.dot_general(
        screen_rows, con_pairs, (((1,), (1,)), ((), ())), preferred_element_type=jnp.float32
    ).astype(jnp.bfloat16)
    partial_sum = jnp.dot(val_pairs, interim, preferred_element_type=jnp.float32)
    partial_sum = partial_sum.reshape(val_count, val_count, con_count, con_count).transpose(
        0, 2, 1, 3
    )
    return partial_sum.reshape(val_count * con_count, val_count * con_count)


def shards(valence_bands, conduction_bands, screened, pair_list, transfer_index, owner_map):
    groups = lax.axis_size("pb")
    rows_split = lax.axis_size("row")
    device = lax.axis_index("pb")
    val_all, con_local = (
        lax.all_gather(valence_bands, "pb", axis=0, tiled=True),
        lax.all_gather(conduction_bands, "pb", axis=0, tiled=True),
    )
    slot_table = rank_table(transfer_index[:, 0], groups, MOST)
    own_slots = lax.dynamic_index_in_dim(slot_table, device, 0, keepdims=False)
    live_pair = jnp.maximum(own_slots, 0)
    slot_first = jnp.take(owner_map, jnp.take(pair_list[:, 0], live_pair))
    slot_second = jnp.take(owner_map, jnp.take(pair_list[:, 1], live_pair))
    val_first = jnp.take(val_all, slot_first, axis=0)
    val_second = jnp.take(val_all, slot_second, axis=0)
    con_full = lax.all_gather(con_local, "row", axis=2, tiled=True)
    con_first = jnp.take(con_full, slot_first, axis=0)
    con_second = jnp.take(con_full, slot_second, axis=0)
    screen_rows = screened[0]

    def one_slot(operands):
        return pair_kernel(operands[0], operands[1], operands[2], operands[3], screen_rows)

    partials = lax.map(one_slot, (val_first, val_second, con_first, con_second))
    shares = lax.psum_scatter(partials, "row", scatter_dimension=1, tiled=True).astype(jnp.bfloat16)
    band_rows = shares.shape[1]
    mirror_table = rank_table(jnp.take(owner_map, pair_list[:, 1]), groups, PAIR_DEV)
    flat_slots = slot_table.reshape(-1)
    own_direct = device * PAIR_DEV + jnp.arange(PAIR_DEV, dtype=jnp.int32)
    own_mirror = lax.dynamic_index_in_dim(mirror_table, device, 0, keepdims=False)
    wanted = jnp.concatenate([own_direct, own_mirror])
    select = (wanted[:, None] == flat_slots[None, :]).astype(jnp.bfloat16)
    arrived = jnp.einsum(
        "ji,ixy->jxy",
        select,
        lax.all_gather(shares, "pb", axis=0, tiled=True),
        preferred_element_type=jnp.float32,
    )
    direct = arrived[:PAIR_DEV].astype(jnp.bfloat16)
    mirror_rows = arrived[PAIR_DEV:].astype(jnp.bfloat16)
    turned = jnp.transpose(mirror_rows, (0, 2, 1)).reshape(
        PAIR_DEV, rows_split, band_rows, band_rows
    )
    swapped = lax.all_to_all(turned, "row", split_axis=1, concat_axis=3, tiled=True)
    mirror = swapped.reshape(PAIR_DEV, band_rows, band_rows * rows_split)
    return (direct, mirror)


def solution(mesh):
    in_specs = (P("pb", None, "row"), P("pb", None, "row"), P("pb", "row", None), P(), P(), P())
    out_specs = (P("pb", "row", None), P("pb", "row", None))
    return jax.shard_map(shards, mesh=mesh, in_specs=in_specs, out_specs=out_specs, check_vma=False)
```

profile of v0, /device:TPU:0, one launch (start us, length us, event | category | flops | bytes accessed | tf_op | source)
XLA Modules:
  0.0 460.9 jit_solution(9152695233821279163)
XLA Ops:
  7.2 12.9 %all_gather.13 = bf16[8,20,1024]{2,1,0:T(8,128)(2,1)} all-gather(bf16[1,20,1024]{2,1,0:T(8,128)(2,1)} %param.17), channel_id=1, replica_groups=mesh['pb'=8,'row'=4] {'pb'}, dimensions={0}, use_global_device_ids=true | all-gather | bytes 368640 | tf_op jit(solution)/shard_map/all_gather | solution.py:48
  24.9 8.8 %all_gather.12 = bf16[8,20,1024]{2,1,0:T(8,128)(2,1)S(1)} all-gather(bf16[1,20,1024]{2,1,0:T(8,128)(2,1)} %param.16), channel_id=1, replica_groups=mesh['pb'=8,'row'=4] {'pb'}, dimensions={0}, use_global_device_ids=true | all-gather | bytes 368640 | tf_op jit(solution)/shard_map/all_gather | solution.py:47
  37.8 19.8 %all-gather.3.cloned.1.call-done = bf16[8,20,4096]{2,1,0:T(8,128)(2,1)} async-done(((bf16[8,20,1024]{2,1,0:T(8,128)(2,1)}), bf16[8,20,4096]{2,1,0:T(8,128)(2,1)}) %all-gather.3.cloned.1.call-update) | async-done | bytes 1310736 | tf_op jit(solution)/shard_map/all_gather | solution.py:57
  57.6 2.1 gather_fusion.8
  59.8 1.2 broadcast_select_fusion
  61.6 1.2 broadcast_select_fusion.1
  62.8 156.2 %while.10 = (s32[]{:T(128)}, f32[6,400,400]{1,2,0:T(8,128)}, bf16[6,20,1024]{2,1,0:T(8,128)(2,1)}, bf16[6,20,1024]{2,1,0:T(8,128)(2,1)}, bf16[6,20,4096]{2,1,0:T...) while((s32[]{:T(128)}, f32[6,400,400]{1,2,0:T(8,128)}, ...), condition=%wide.region_5.10_spmd, body=%wide.region_4.9_spmd.sunk | while | flops 3687833600 | bytes 31480412 | solution.py:65
  62.8 1.1 bitcast_convert_fusion.6
  63.9 2.6 multiply_convert_fusion.3
  66.5 3.9 convert_element_type.89
  70.4 7.0 %convolution_convert_fusion.3 = bf16[400,1024]{1,0:T(8,128)(2,1)} fusion(bf16[400,4096]{1,0:T(8,128)(2,1)S(1)} %convert_element_type.89, bf16[1024,4096]{1,0:T(8,128)(2,1)} %get-tuple-element.156), kind=kOutput, calls=%fused_computation.12.clone.1 | convolution fusion | flops 3355852800 | bytes 12484608 | tf_op jit(solution)/shard_map/while/body/eval_jaxpr/dot_general | solution.py:32
  77.4 1.2 reshape.284
  78.7 0.8 bitcast_convert_fusion.7
  79.5 4.5 convolution_bitcast_fusion.2
  84.0 3.6 broadcast_in_dim.75
  87.9 1.0 constant_dynamic-update-slice_fusion.2
  88.9 1.1 bitcast_convert_fusion.6
  89.9 2.6 multiply_convert_fusion.3
  92.6 3.9 convert_element_type.89
  96.4 7.0 %convolution_convert_fusion.3 = bf16[400,1024]{1,0:T(8,128)(2,1)} fusion(bf16[400,4096]{1,0:T(8,128)(2,1)S(1)} %convert_element_type.89, bf16[1024,4096]{1,0:T(8,128)(2,1)} %get-tuple-element.156), kind=kOutput, calls=%fused_computation.12.clone.1 | convolution fusion | flops 3355852800 | bytes 12484608 | tf_op jit(solution)/shard_map/while/body/eval_jaxpr/dot_general | solution.py:32
  103.5 1.2 reshape.284
  105.6 4.5 convolution_bitcast_fusion.2
  110.0 3.6 broadcast_in_dim.75
  113.9 1.0 constant_dynamic-update-slice_fusion.2
  114.9 1.1 bitcast_convert_fusion.6
  116.0 2.6 multiply_convert_fusion.3
  118.6 3.9 convert_element_type.89
  122.5 7.0 %convolution_convert_fusion.3 = bf16[400,1024]{1,0:T(8,128)(2,1)} fusion(bf16[400,4096]{1,0:T(8,128)(2,1)S(1)} %convert_element_type.89, bf16[1024,4096]{1,0:T(8,128)(2,1)} %get-tuple-element.156), kind=kOutput, calls=%fused_computation.12.clone.1 | convolution fusion | flops 3355852800 | bytes 12484608 | tf_op jit(solution)/shard_map/while/body/eval_jaxpr/dot_general | solution.py:32
  129.5 1.2 reshape.284
  131.6 4.5 convolution_bitcast_fusion.2
  136.0 3.6 broadcast_in_dim.75
  139.9 1.0 constant_dynamic-update-slice_fusion.2
  140.9 1.1 bitcast_convert_fusion.6
  142.0 2.6 multiply_convert_fusion.3
  144.6 3.9 convert_element_type.89
  148.5 7.0 %convolution_convert_fusion.3 = bf16[400,1024]{1,0:T(8,128)(2,1)} fusion(bf16[400,4096]{1,0:T(8,128)(2,1)S(1)} %convert_element_type.89, bf16[1024,4096]{1,0:T(8,128)(2,1)} %get-tuple-element.156), kind=kOutput, calls=%fused_computation.12.clone.1 | convolution fusion | flops 3355852800 | bytes 12484608 | tf_op jit(solution)/shard_map/while/body/eval_jaxpr/dot_general | solution.py:32
  155.5 1.2 reshape.284
  157.6 4.5 convolution_bitcast_fusion.2
  162.1 3.6 broadcast_in_dim.75
  166.0 1.0 constant_dynamic-update-slice_fusion.2
  167.0 1.1 bitcast_convert_fusion.6
  168.0 2.6 multiply_convert_fusion.3
  170.6 3.9 convert_element_type.89
  174.5 7.0 %convolution_convert_fusion.3 = bf16[400,1024]{1,0:T(8,128)(2,1)} fusion(bf16[400,4096]{1,0:T(8,128)(2,1)S(1)} %convert_element_type.89, bf16[1024,4096]{1,0:T(8,128)(2,1)} %get-tuple-element.156), kind=kOutput, calls=%fused_computation.12.clone.1 | convolution fusion | flops 3355852800 | bytes 12484608 | tf_op jit(solution)/shard_map/while/body/eval_jaxpr/dot_general | solution.py:32
  181.6 1.2 reshape.284
  183.7 4.5 convolution_bitcast_fusion.2
  188.1 3.6 broadcast_in_dim.75
  192.0 1.0 constant_dynamic-update-slice_fusion.2
  193.0 1.1 bitcast_convert_fusion.6
  194.0 2.6 multiply_convert_fusion.3
  196.7 3.9 convert_element_type.89
  200.5 7.0 %convolution_convert_fusion.3 = bf16[400,1024]{1,0:T(8,128)(2,1)} fusion(bf16[400,4096]{1,0:T(8,128)(2,1)S(1)} %convert_element_type.89, bf16[1024,4096]{1,0:T(8,128)(2,1)} %get-tuple-element.156), kind=kOutput, calls=%fused_computation.12.clone.1 | convolution fusion | flops 3355852800 | bytes 12484608 | tf_op jit(solution)/shard_map/while/body/eval_jaxpr/dot_general | solution.py:32
  207.6 1.2 reshape.284
  209.7 4.5 convolution_bitcast_fusion.2
  214.1 3.6 broadcast_in_dim.75
  218.0 1.0 constant_dynamic-update-slice_fusion.2
  219.0 169.8 %all-reduce.2 = bf16[6,400,400]{1,2,0:T(8,128)(2,1)S(1)} all-reduce(f32[6,400,400]{1,2,0:T(8,128)} %get-tuple-element.43), channel_id=2, replica_groups=mesh['pb'=8,'row'=4] {'row'}, use_global_device_ids=true, to_apply=%region_6.11.clone | all-reduce | flops 960000 | bytes 5760000
  388.8 1.1 dynamic-slice_convert_fusion
  391.4 36.1 %all-gather.5.cloned.1.call-done = bf16[48,100,400]{1,2,0:T(8,128)(2,1)} async-done(((bf16[6,100,400]{1,2,0:T(8,128)(2,1)}), bf16[48,100,400]{1,2,0:T(8,128)(2,1)}) %all-gather.5.cloned.1.call-update) | async-done | bytes 3840016 | tf_op jit(solution)/shard_map/all_gather | solution.py:77
  427.5 8.4 %copy.27 = bf16[48,100,400]{2,0,1:T(8,128)(2,1)} copy(bf16[48,100,400]{1,2,0:T(8,128)(2,1)} %all-gather.5.cloned.1.call-done) | data formatting | bytes 7680000 | tf_op jit(solution)/shard_map/all_gather | solution.py:77
  435.9 3.2 convolution_convert_fusion.1
  439.1 1.0 slice_bitcast_fusion
  440.4 12.5 %all_to_all.15 = bf16[2,4,100,100]{2,0,3,1:T(2,128)(2,1)S(1)} all-to-all(bf16[2,4,100,100]{2,0,3,1:T(2,128)(2,1)S(1)} %copy.28), channel_id=1, replica_groups=mesh['pb'=8,'row'=4] {'row'}, dimensions={1} | all-to-all | bytes 320000 | tf_op jit(solution)/shard_map/all_to_all | solution.py:85
  452.9 1.2 copy.29
  (65 shorter events, 16.5 us)
Async XLA Ops:
  7.2 16.4 %copy-start = (s32[8]{0:T(128)S(1)}, s32[8]{0:T(128)}, u32[]{:S(2)}) copy-start(s32[8]{0:T(128)} %param.21) | copy-start | bytes 100
  7.2 27.8 %copy-start.3 = (u32[32]{0:T(128)S(1)}, u32[32]{0:T(128)}, u32[]{:S(2)}) copy-start(u32[32]{0:T(128)} %constant.110) | copy-start | bytes 388
  7.2 50.4 %all-gather.3.cloned.1.call-start = ((), (), s32[]{:S(2)}) async-start(), calls=%async_computation.1 | async-start | bytes 1966080 | tf_op jit(solution)/shard_map/all_gather | solution.py:57
  20.2 407.3 %all-gather.5.cloned.1.call-start = ((), (), s32[]{:S(2)}) async-start(), calls=%async_computation.2 | async-start | bytes 5529600 | tf_op jit(solution)/shard_map/all_gather | solution.py:77
  57.6 3.4 copy-start.1
  219.0 171.7 %copy-start.2 = (s32[16,2]{0,1:T(2,128)S(1)}, s32[16,2]{0,1:T(2,128)}, u32[]{:S(2)}) copy-start(s32[16,2]{0,1:T(2,128)} %param.19) | copy-start | bytes 388
Sparse Core Ops, SparseCore 0:
  20.3 37.2 all-gather.2
  390.1 37.3 all-gather.4
where the time goes:
time: 463 us; the launch traced here: 461 us
  blocking collectives  204 us (44%)
  local copies, waits for them, and re-layouts  80 us (17%)
  matrix products  72.2 us (16%)
  waiting for transfers between devices  55.9 us (12%)
  other arithmetic  33.6 us (7%)
  between operations  14.9 us (3%)
    unnamed x1, blocking collectives  170 us
    dot_general x6, matrix products, pair_kernel(): lax.dot_general(screen_rows, con_pairs, (((1,), (1,)), ((), ())), preferr...  42.1 us
    all_gather x1, waiting for transfers between devices, shards(): lax.all_gather(shares, 'pb', axis=0, tiled=True)  36.1 us
    dot_general x6, matrix products, pair_kernel(): jnp.dot(val_pairs, interim, preferred_element_type=jnp.float32)  26.8 us
    convert_element_type x6, local copies, waits for them, and re-layouts, pair_kernel(): con_pairs.reshape(con_count * con_count, con_first.shape[1])  23.3 us
    broadcast_in_dim x6, local copies, waits for them, and re-layouts, shards(): partials = lax.map(one_slot, (val_first, val_second, con_first, con_second))  21.6 us
    all_gather x1, waiting for transfers between devices, shards(): con_full = lax.all_gather(con_local, 'row', axis=2, tiled=True)  19.8 us
    convert_element_type x6, other arithmetic, pair_kernel(): con_pairs.reshape(con_count * con_count, con_first.shape[1])  15.6 us
  transfers between devices with their start and end apart: 2, of which 2 were waited for; matrix products, arithmetic and copies ran while one was open for 2% of the time, Pallas kernels for 0%

commit v1 on v0

--- a/solution.py
+++ b/solution.py
@@ -5,6 +5,18 @@
 
 PAIR_DEV = 2
 MOST = 6
+
+
+def product_in_turn(shard, axis, dim, contribution):
+    size, position, rows = (lax.axis_size(axis), lax.axis_index(axis), shard.shape[dim])
+    ahead = [(i, (i + 1) % size) for i in range(size)]
+    carried, total = (shard, None)
+    for step in range(size):
+        coming = lax.ppermute(carried, axis, ahead) if step < size - 1 else None
+        take_in = contribution(carried, (position - step) % size * rows)
+        total = take_in if total is None else total + take_in
+        carried = coming
+    return total
 
 
 def rank_table(labels, groups, slots_per):
@@ -71,11 +83,16 @@
     own_mirror = lax.dynamic_index_in_dim(mirror_table, device, 0, keepdims=False)
     wanted = jnp.concatenate([own_direct, own_mirror])
     select = (wanted[:, None] == flat_slots[None, :]).astype(jnp.bfloat16)
-    arrived = jnp.einsum(
-        "ji,ixy->jxy",
-        select,
-        lax.all_gather(shares, "pb", axis=0, tiled=True),
-        preferred_element_type=jnp.float32,
+    arrived = product_in_turn(
+        shares,
+        "pb",
+        0,
+        lambda own_block, start: jnp.einsum(
+            "ji,ixy->jxy",
+            lax.dynamic_slice_in_dim(select, start, own_block.shape[0], axis=1),
+            own_block,
+            preferred_element_type=jnp.float32,
+        ),
     )
     direct = arrived[:PAIR_DEV].astype(jnp.bfloat16)
     mirror_rows = arrived[PAIR_DEV:].astype(jnp.bfloat16)

time: 463 us -> 486 us (1.050)
  waiting for transfers between devices: 55.9 us -> 77.2 us
  local copies, waits for them, and re-layouts: 80 us -> 85.2 us
    ppermute x0 -> x7, waiting for transfers between devices: none -> 57.2 us  [product_in_turn(): coming = lax.ppermute(carried, axis, ahead) if step < size - 1 else None]
    all_gather x1 -> x0, waiting for transfers between devices: 36.1 us -> none  [shards(): lax.all_gather(shares, 'pb', axis=0, tiled=True)]
    ppermute x0 -> x7, local copies, waits for them, and re-layouts: none -> 13.2 us  [product_in_turn(): coming = lax.ppermute(carried, axis, ahead) if step < size - 1 else None]
    all_gather x1 -> x0, local copies, waits for them, and re-layouts: 8.41 us -> none  [shards(): lax.all_gather(shares, 'pb', axis=0, tiled=True)]
  transfers between devices with their start and end apart: 2 -> 8, of which waited for: 2 -> 8; matrix products, arithmetic and copies ran while one was open for 2% -> 5% of each run, Pallas kernels for 0% -> 0%
where the time goes in v1:
time: 486 us; the launch traced here: 484 us
  blocking collectives  200 us (41%)
  local copies, waits for them, and re-layouts  85.2 us (18%)
  waiting for transfers between devices  77.2 us (16%)
  matrix products  72.7 us (15%)
  other arithmetic  33.7 us (7%)
  between operations  15.2 us (3%)
    unnamed x1, blocking collectives  169 us
    ppermute x7, waiting for transfers between devices, product_in_turn(): coming = lax.ppermute(carried, axis, ahead) if step < size - 1 else None  57.2 us
    dot_general x6, matrix products, pair_kernel(): lax.dot_general(screen_rows, con_pairs, (((1,), (1,)), ((), ())), preferr...  42.2 us
    dot_general x6, matrix products, pair_kernel(): jnp.dot(val_pairs, interim, preferred_element_type=jnp.float32)  27 us
    convert_element_type x6, local copies, waits for them, and re-layouts, pair_kernel(): con_pairs.reshape(con_count * con_count, con_first.shape[1])  23.3 us
    broadcast_in_dim x6, local copies, waits for them, and re-layouts, shards(): partials = lax.map(one_slot, (val_first, val_second, con_first, con_second))  21.6 us
    all_gather x1, waiting for transfers between devices, shards(): con_full = lax.all_gather(con_local, 'row', axis=2, tiled=True)  20 us
    convert_element_type x6, other arithmetic, pair_kernel(): con_pairs.reshape(con_count * con_count, con_first.shape[1])  15.6 us
  transfers between devices with their start and end apart: 8, of which 8 were waited for; matrix products, arithmetic and copies ran while one was open for 5% of the time, Pallas kernels for 0%

profile of v1, /device:TPU:0, one launch (start us, length us, event | category | flops | bytes accessed | tf_op | source)
XLA Modules:
  0.0 484.3 jit_solution(7427244148462633927)
XLA Ops:
  7.2 12.9 %all_gather.10 = bf16[8,20,1024]{2,1,0:T(8,128)(2,1)} all-gather(bf16[1,20,1024]{2,1,0:T(8,128)(2,1)} %param.17), channel_id=1, replica_groups=mesh['pb'=8,'row'=4] {'pb'}, dimensions={0}, use_global_device_ids=true | all-gather | bytes 368640 | tf_op jit(solution)/shard_map/all_gather | solution.py:60
  24.9 8.7 %all_gather.9 = bf16[8,20,1024]{2,1,0:T(8,128)(2,1)S(1)} all-gather(bf16[1,20,1024]{2,1,0:T(8,128)(2,1)S(1)} %copy-done.5), channel_id=1, replica_groups=mesh['pb'=8,'row'=4] {'pb'}, dimensions={0}, use_global_device_ids=true | all-gather | bytes 368640 | tf_op jit(solution)/shard_map/all_gather | solution.py:59
  37.6 20.0 %all-gather.2.cloned.1.call-done = bf16[8,20,4096]{2,1,0:T(8,128)(2,1)} async-done(((bf16[8,20,1024]{2,1,0:T(8,128)(2,1)}), bf16[8,20,4096]{2,1,0:T(8,128)(2,1)}) %all-gather.2.cloned.1.call-update) | async-done | bytes 1310736 | tf_op jit(solution)/shard_map/all_gather | solution.py:69
  57.6 2.1 gather_fusion.8
  59.8 1.2 broadcast_select_fusion
  61.6 1.2 broadcast_select_fusion.1
  62.8 156.4 %while.10 = (s32[]{:T(128)}, f32[6,400,400]{1,2,0:T(8,128)}, bf16[6,20,1024]{2,1,0:T(8,128)(2,1)}, bf16[6,20,1024]{2,1,0:T(8,128)(2,1)}, bf16[6,20,4096]{2,1,0:T...) while((s32[]{:T(128)}, f32[6,400,400]{1,2,0:T(8,128)}, ...), condition=%wide.region_5.10_spmd, body=%wide.region_4.9_spmd.sunk | while | flops 3687833600 | bytes 31480412 | solution.py:77
  62.8 1.1 bitcast_convert_fusion.6
  63.9 2.6 multiply_convert_fusion.3
  66.5 3.9 convert_element_type.89
  70.4 7.0 %convolution_convert_fusion.2 = bf16[400,1024]{1,0:T(8,128)(2,1)} fusion(bf16[400,4096]{1,0:T(8,128)(2,1)S(1)} %convert_element_type.89, bf16[1024,4096]{1,0:T(8,128)(2,1)} %get-tuple-element.156), kind=kOutput, calls=%fused_computation.12.clone.1 | convolution fusion | flops 3355852800 | bytes 12484608 | tf_op jit(solution)/shard_map/while/body/eval_jaxpr/dot_general | solution.py:44
  77.4 1.2 reshape.291
  79.5 4.5 convolution_bitcast_fusion.2
  84.0 3.6 broadcast_in_dim.75
  90.0 2.6 multiply_convert_fusion.3
  92.6 3.9 convert_element_type.89
  96.5 7.0 %convolution_convert_fusion.2 = bf16[400,1024]{1,0:T(8,128)(2,1)} fusion(bf16[400,4096]{1,0:T(8,128)(2,1)S(1)} %convert_element_type.89, bf16[1024,4096]{1,0:T(8,128)(2,1)} %get-tuple-element.156), kind=kOutput, calls=%fused_computation.12.clone.1 | convolution fusion | flops 3355852800 | bytes 12484608 | tf_op jit(solution)/shard_map/while/body/eval_jaxpr/dot_general | solution.py:44
  103.5 1.2 reshape.291
  105.6 4.5 convolution_bitcast_fusion.2
  110.1 3.6 broadcast_in_dim.75
  115.0 1.1 bitcast_convert_fusion.6
  116.0 2.6 multiply_convert_fusion.3
  118.7 3.9 convert_element_type.89
  122.5 7.0 %convolution_convert_fusion.2 = bf16[400,1024]{1,0:T(8,128)(2,1)} fusion(bf16[400,4096]{1,0:T(8,128)(2,1)S(1)} %convert_element_type.89, bf16[1024,4096]{1,0:T(8,128)(2,1)} %get-tuple-element.156), kind=kOutput, calls=%fused_computation.12.clone.1 | convolution fusion | flops 3355852800 | bytes 12484608 | tf_op jit(solution)/shard_map/while/body/eval_jaxpr/dot_general | solution.py:44
  129.6 1.2 reshape.291
  131.7 4.5 convolution_bitcast_fusion.2
  136.2 3.6 broadcast_in_dim.75
  142.1 2.6 multiply_convert_fusion.3
  144.7 3.9 convert_element_type.89
  148.6 7.0 %convolution_convert_fusion.2 = bf16[400,1024]{1,0:T(8,128)(2,1)} fusion(bf16[400,4096]{1,0:T(8,128)(2,1)S(1)} %convert_element_type.89, bf16[1024,4096]{1,0:T(8,128)(2,1)} %get-tuple-element.156), kind=kOutput, calls=%fused_computation.12.clone.1 | convolution fusion | flops 3355852800 | bytes 12484608 | tf_op jit(solution)/shard_map/while/body/eval_jaxpr/dot_general | solution.py:44
  155.6 1.2 reshape.291
  157.7 4.5 convolution_bitcast_fusion.2
  162.2 3.6 broadcast_in_dim.75
  168.1 2.6 multiply_convert_fusion.3
  170.7 3.9 convert_element_type.89
  174.6 7.0 %convolution_convert_fusion.2 = bf16[400,1024]{1,0:T(8,128)(2,1)} fusion(bf16[400,4096]{1,0:T(8,128)(2,1)S(1)} %convert_element_type.89, bf16[1024,4096]{1,0:T(8,128)(2,1)} %get-tuple-element.156), kind=kOutput, calls=%fused_computation.12.clone.1 | convolution fusion | flops 3355852800 | bytes 12484608 | tf_op jit(solution)/shard_map/while/body/eval_jaxpr/dot_general | solution.py:44
  181.7 1.2 reshape.291
  183.8 4.5 convolution_bitcast_fusion.2
  188.3 3.6 broadcast_in_dim.75
  193.1 1.1 bitcast_convert_fusion.6
  194.2 2.6 multiply_convert_fusion.3
  196.8 3.9 convert_element_type.89
  200.7 7.0 %convolution_convert_fusion.2 = bf16[400,1024]{1,0:T(8,128)(2,1)} fusion(bf16[400,4096]{1,0:T(8,128)(2,1)S(1)} %convert_element_type.89, bf16[1024,4096]{1,0:T(8,128)(2,1)} %get-tuple-element.156), kind=kOutput, calls=%fused_computation.12.clone.1 | convolution fusion | flops 3355852800 | bytes 12484608 | tf_op jit(solution)/shard_map/while/body/eval_jaxpr/dot_general | solution.py:44
  207.7 1.2 reshape.291
  209.8 4.5 convolution_bitcast_fusion.2
  214.3 3.6 broadcast_in_dim.75
  219.2 169.3 %all-reduce.2 = bf16[6,400,400]{1,2,0:T(8,128)(2,1)S(1)} all-reduce(f32[6,400,400]{1,2,0:T(8,128)} %get-tuple-element.43), channel_id=2, replica_groups=mesh['pb'=8,'row'=4] {'row'}, use_global_device_ids=true, to_apply=%region_6.11.clone | all-reduce | flops 960000 | bytes 5760000
  389.5 9.8 %collective-permute-done = bf16[6,100,400]{1,2,0:T(8,128)(2,1)S(1)} collective-permute-done((bf16[6,100,400]{1,2,0:T(8,128)(2,1)S(1)}, bf16[6,100,400]{1,2,0:T(8,128)(2,1)S(1)}, u32[]{:S(2)}, u32[]{:S(2)}) %collective-permute-start) | collective-permute-done | bytes 480032 | tf_op jit(solution)/shard_map/ppermute | solution.py:15
  399.5 10.3 %collective-permute-done.1 = bf16[6,100,400]{1,2,0:T(8,128)(2,1)S(1)} collective-permute-done((bf16[6,100,400]{1,2,0:T(8,128)(2,1)S(1)}, bf16[6,100,400]{1,2,0:T(8,128)(2,1)S(1)}, u32[]{:S(2)}, u32[]{:S(2)}) %collective-permute-start.1) | collective-permute-done | bytes 480032 | tf_op jit(solution)/shard_map/ppermute | solution.py:15
  410.4 9.9 %collective-permute-done.2 = bf16[6,100,400]{1,2,0:T(8,128)(2,1)} collective-permute-done((bf16[6,100,400]{1,2,0:T(8,128)(2,1)S(1)}, bf16[6,100,400]{1,2,0:T(8,128)(2,1)}, u32[]{:S(2)}, u32[]{:S(2)}) %collective-permute-start.2) | collective-permute-done | bytes 480032 | tf_op jit(solution)/shard_map/ppermute | solution.py:15
  420.4 1.2 copy.48
  422.1 2.2 copy.49
  424.3 6.8 %collective-permute-done.3 = bf16[6,100,400]{1,2,0:T(8,128)(2,1)} collective-permute-done((bf16[6,100,400]{1,2,0:T(8,128)(2,1)}, bf16[6,100,400]{1,2,0:T(8,128)(2,1)}, u32[]{:S(2)}, u32[]{:S(2)}) %collective-permute-start.3) | collective-permute-done | bytes 480032 | tf_op jit(solution)/shard_map/ppermute | solution.py:15
  431.6 1.2 copy.50
  433.2 2.1 copy.51
  435.4 6.5 %collective-permute-done.4 = bf16[6,100,400]{1,2,0:T(8,128)(2,1)} collective-permute-done((bf16[6,100,400]{1,2,0:T(8,128)(2,1)}, bf16[6,100,400]{1,2,0:T(8,128)(2,1)}, u32[]{:S(2)}, u32[]{:S(2)}) %collective-permute-start.4) | collective-permute-done | bytes 480032 | tf_op jit(solution)/shard_map/ppermute | solution.py:15
  442.3 2.1 copy.52
  444.9 2.1 copy.53
  447.1 5.5 %collective-permute-done.5 = bf16[6,100,400]{1,2,0:T(8,128)(2,1)S(1)} collective-permute-done((bf16[6,100,400]{1,2,0:T(8,128)(2,1)}, bf16[6,100,400]{1,2,0:T(8,128)(2,1)S(1)}, u32[]{:S(2)}, u32[]{:S(2)}) %collective-permute-start.5) | collective-permute-done | bytes 480032 | tf_op jit(solution)/shard_map/ppermute | solution.py:15
  453.0 1.2 copy.54
  454.7 8.5 %collective-permute-done.6 = bf16[6,100,400]{1,2,0:T(8,128)(2,1)} collective-permute-done((bf16[6,100,400]{1,2,0:T(8,128)(2,1)S(1)}, bf16[6,100,400]{1,2,0:T(8,128)(2,1)}, u32[]{:S(2)}, u32[]{:S(2)}) %collective-permute-start.6) | collective-permute-done | bytes 480032 | tf_op jit(solution)/shard_map/ppermute | solution.py:15
  463.1 2.1 copy.55
  467.1 9.2 %all_to_all.15 = bf16[2,4,100,100]{2,0,3,1:T(2,128)(2,1)S(1)} all-to-all(bf16[2,4,100,100]{2,0,3,1:T(2,128)(2,1)S(1)} %copy.56), channel_id=1, replica_groups=mesh['pb'=8,'row'=4] {'row'}, dimensions={1} | all-to-all | bytes 320000 | tf_op jit(solution)/shard_map/all_to_all | solution.py:102
  476.3 1.2 copy.57
  (99 shorter events, 31.2 us)
Async XLA Ops:
  7.2 16.4 %copy-start = (s32[8]{0:T(128)S(1)}, s32[8]{0:T(128)}, u32[]{:S(2)}) copy-start(s32[8]{0:T(128)} %param.21) | copy-start | bytes 100
  7.2 17.7 %copy-start.5 = (bf16[1,20,1024]{2,1,0:T(8,128)(2,1)S(1)}, bf16[1,20,1024]{2,1,0:T(8,128)(2,1)}, u32[]{:S(2)}) copy-start(bf16[1,20,1024]{2,1,0:T(8,128)(2,1)} %param.16) | copy-start | bytes 122884
  7.2 50.4 %all-gather.2.cloned.1.call-start = ((), (), s32[]{:S(2)}) async-start(), calls=%async_computation.1 | async-start | bytes 1966080 | tf_op jit(solution)/shard_map/all_gather | solution.py:69
  20.2 14.5 %copy-start.7 = (u32[32]{0:T(128)S(1)}, u32[32]{0:T(128)}, u32[]{:S(2)}) copy-start(u32[32]{0:T(128)} %constant.170) | copy-start | bytes 388
  57.6 3.4 copy-start.1
  219.2 180.1 %copy-start.6 = (s32[16,2]{0,1:T(2,128)S(1)}, s32[16,2]{0,1:T(2,128)}, u32[]{:S(2)}) copy-start(s32[16,2]{0,1:T(2,128)} %param.19) | copy-start | bytes 388
  388.7 10.5 %collective-permute-start = (bf16[6,100,400]{1,2,0:T(8,128)(2,1)S(1)}, bf16[6,100,400]{1,2,0:T(8,128)(2,1)S(1)}, u32[]{:S(2)}, u32[]{:S(2)}) collective-permute-start(bf16[6,100,400]{1,2,0:T(8,128)(2,1)S(1)} %dynamic-slice_convert_fusion), channel_id=1, source_target_pairs={{0,4},{4,8},{8,12},{12,16},{16,20},{20,24},{24,28},{28,0},{1,5},{5... | collective-permute-start | bytes 1440008 | tf_op jit(solution)/shard_map/ppermute | solution.py:15
  399.3 21.1 %copy-start.4 = (bf16[6,100,400]{1,2,0:T(8,128)(2,1)}, bf16[6,100,400]{1,2,0:T(8,128)(2,1)S(1)}, u32[]{:S(2)}) copy-start(bf16[6,100,400]{1,2,0:T(8,128)(2,1)S(1)} %collective-permute-done) | copy-start | bytes 1440004
  399.3 10.5 %collective-permute-start.1 = (bf16[6,100,400]{1,2,0:T(8,128)(2,1)S(1)}, bf16[6,100,400]{1,2,0:T(8,128)(2,1)S(1)}, u32[]{:S(2)}, u32[]{:S(2)}) collective-permute-start(bf16[6,100,400]{1,2,0:T(8,128)(2,1)S(1)} %collective-permute-done), channel_id=1, source_target_pairs={{0,4},{4,8},{8,12},{12,16},{16,20},{20,24},{24,28},{28,0},{1,5},{5... | collective-permute-start | bytes 1440008 | tf_op jit(solution)/shard_map/ppermute | solution.py:15
  409.7 10.7 %copy-start.2 = (bf16[6,100,400]{1,2,0:T(8,128)(2,1)}, bf16[6,100,400]{1,2,0:T(8,128)(2,1)S(1)}, u32[]{:S(2)}) copy-start(bf16[6,100,400]{1,2,0:T(8,128)(2,1)S(1)} %collective-permute-done.1) | copy-start | bytes 1440004
  409.7 10.6 %collective-permute-start.2 = (bf16[6,100,400]{1,2,0:T(8,128)(2,1)S(1)}, bf16[6,100,400]{1,2,0:T(8,128)(2,1)}, u32[]{:S(2)}, u32[]{:S(2)}) collective-permute-start(bf16[6,100,400]{1,2,0:T(8,128)(2,1)S(1)} %collective-permute-done.1), channel_id=1, source_target_pairs={{0,4},{4,8},{8,12},{12,16},{16,20},{20,24},{24,28},{28,0},{1,5},{5... | collective-permute-start | bytes 1440008 | tf_op jit(solution)/shard_map/ppermute | solution.py:15
  420.3 10.8 %collective-permute-start.3 = (bf16[6,100,400]{1,2,0:T(8,128)(2,1)}, bf16[6,100,400]{1,2,0:T(8,128)(2,1)}, u32[]{:S(2)}, u32[]{:S(2)}) collective-permute-start(bf16[6,100,400]{1,2,0:T(8,128)(2,1)} %collective-permute-done.2), channel_id=1, source_target_pairs={{0,4},{4,8},{8,12},{12,16},{16,20},{20,24},{24,28},{28,0},{1,5},{5... | collective-permute-start | bytes 1440008 | tf_op jit(solution)/shard_map/ppermute | solution.py:15
  422.0 9.5 %copy-start.3 = (bf16[6,100,400]{1,2,0:T(8,128)(2,1)S(1)}, bf16[6,100,400]{1,2,0:T(8,128)(2,1)}, u32[]{:S(2)}) copy-start(bf16[6,100,400]{1,2,0:T(8,128)(2,1)} %copy-done.2) | copy-start | bytes 1440004
  431.1 10.8 %collective-permute-start.4 = (bf16[6,100,400]{1,2,0:T(8,128)(2,1)}, bf16[6,100,400]{1,2,0:T(8,128)(2,1)}, u32[]{:S(2)}, u32[]{:S(2)}) collective-permute-start(bf16[6,100,400]{1,2,0:T(8,128)(2,1)} %collective-permute-done.3), channel_id=1, source_target_pairs={{0,4},{4,8},{8,12},{12,16},{16,20},{20,24},{24,28},{28,0},{1,5},{5... | collective-permute-start | bytes 1440008 | tf_op jit(solution)/shard_map/ppermute | solution.py:15
  441.9 10.7 %collective-permute-start.5 = (bf16[6,100,400]{1,2,0:T(8,128)(2,1)}, bf16[6,100,400]{1,2,0:T(8,128)(2,1)S(1)}, u32[]{:S(2)}, u32[]{:S(2)}) collective-permute-start(bf16[6,100,400]{1,2,0:T(8,128)(2,1)} %collective-permute-done.4), channel_id=1, source_target_pairs={{0,4},{4,8},{8,12},{12,16},{16,20},{20,24},{24,28},{28,0},{1,5},{5... | collective-permute-start | bytes 1440008 | tf_op jit(solution)/shard_map/ppermute | solution.py:15
  452.6 10.6 %collective-permute-start.6 = (bf16[6,100,400]{1,2,0:T(8,128)(2,1)S(1)}, bf16[6,100,400]{1,2,0:T(8,128)(2,1)}, u32[]{:S(2)}, u32[]{:S(2)}) collective-permute-start(bf16[6,100,400]{1,2,0:T(8,128)(2,1)S(1)} %collective-permute-done.5), channel_id=1, source_target_pairs={{0,4},{4,8},{8,12},{12,16},{16,20},{20,24},{24,28},{28,0},{1,5},{5... | collective-permute-start | bytes 1440008 | tf_op jit(solution)/shard_map/ppermute | solution.py:15
Sparse Core Ops, SparseCore 0:
  20.3 37.2 all-gather.1
